TPU v7x, 32 devices: a whole 2x2x4 slice. The times are simulated.
32 devices in a mesh: dp: 4 (over z), tensor: 8 (over y, x, core).
Axes of the slice: x: 2, y: 2, z: 4, core: 2. Of those that a mesh axis runs over, the one named last changes fastest.
Arguments:
- activations: bfloat16 [3072, 4096], P('dp', 'tensor'), may hold values from -6 to 6
- out_grads_t: bfloat16 [5504, 3072], P('tensor', 'dp'), may hold values from -6 to 6
- in_basis: bfloat16 [4096, 4096], P(None, 'tensor'), may hold values from -0.09375 to 0.09375
- out_basis_t: bfloat16 [5504, 5504], P('tensor'), may hold values from -0.078125 to 0.078125
- query_proj: bfloat16 [4, 5504, 4096], P(None, 'tensor', 'dp'), may hold values from -6 to 6
- eigvals: float32 [5504, 4096], P('tensor', 'dp'), may hold values from 0.05 to 5
- damping: float32 [1], replicated, may hold values from 0.05 to 0.2
- lengths: int32 [24], P('dp'), may hold values from 1 to 128, 1920 in all
Outputs:
- scores: float32 [24, 4], P('dp')
Inputs may be any that keep to these rules, and one draw needn't show every extreme that they name: `lengths`: the largest token count is exactly 128.
All inputs are finite; a program needn't handle non-finite values. No bound on the sum of `lengths` on one device may be relied on, other than what follows from the above.
Results may differ from a plain program's by a relative error of at most 0.006.
Values may be sent and summed in bfloat16 or wider, within the bound.
A program may use at most 128 MiB of HBM per device.

v0:
```python
import jax
import jax.numpy as jnp
from jax import lax
from jax.sharding import PartitionSpec as P


def local(activations, out_grads_t, in_basis, out_basis_t, query_proj, eigvals, damping, lengths):
    bf16, f32 = (jnp.bfloat16, jnp.float32)
    seq_count = lengths.shape[0]
    full_act = lax.all_gather(activations, "tensor", axis=1, tiled=True)
    token_rows = full_act.shape[0]
    seq_len = token_rows // seq_count
    act_local = jnp.dot(full_act, in_basis, preferred_element_type=f32).astype(bf16)
    act_full = lax.all_gather(act_local, "tensor", axis=1, tiled=True)
    features = act_full.shape[1]
    act_proj = lax.all_to_all(act_full, "dp", split_axis=1, concat_axis=0, tiled=True)
    grad_full = jnp.dot(
        out_basis_t,
        lax.all_gather(out_grads_t, "tensor", axis=0, tiled=True),
        preferred_element_type=f32,
    )
    position = lax.broadcasted_iota(jnp.int32, (seq_count, seq_len), 1)
    keep = (position < lengths[:, None]).astype(f32).reshape(1, token_rows)
    grad_local = (grad_full * keep).astype(bf16)
    grad_proj = lax.all_gather(grad_local, "dp", axis=1, tiled=True)
    scaled = (query_proj.astype(f32) / (eigvals + damping[0])).astype(bf16)
    mixed = jnp.einsum("td,qjd->qjt", act_proj, scaled, preferred_element_type=f32)
    weighted = mixed * grad_proj.astype(f32)[None, :, :]
    query_count, width, tokens = weighted.shape
    partial_value = jnp.sum(
        weighted.reshape(query_count, width, tokens // seq_len, seq_len), axis=(1, 3)
    ).T
    totals = lax.psum(partial_value, ("dp", "tensor"))
    mine = lax.dynamic_slice_in_dim(totals, lax.axis_index("dp") * seq_count, seq_count, 0)
    norm_factor = (features * out_basis_t.shape[1] * seq_len) ** (-0.5)
    return mine * norm_factor


def solution(mesh):
    placed = (
        P("dp", "tensor"),
        P("tensor", "dp"),
        P(None, "tensor"),
        P("tensor", None),
        P(None, "tensor", "dp"),
        P("tensor", "dp"),
        P(),
        P("dp"),
    )
    return jax.shard_map(
        local, mesh=mesh, in_specs=placed, out_specs=P("dp", None), check_vma=False
    )
```

profile of v0, /device:TPU:0, one launch (start us, length us, event | category | flops | bytes accessed | tf_op | source)
XLA Modules:
  0.0 405.4 jit_solution(16750571598699061149)
XLA Ops:
  6.5 0.0 all-gather.5.cloned.1.call-start
  6.5 0.7 all-gather.5.cloned.1.call-update
  7.3 0.0 all-gather.7.cloned.1.call-start
  7.3 51.2 %all-gather.5.cloned.1.call-done = bf16[768,4096]{1,0:T(8,128)(2,1)} async-done(((bf16[768,512]{1,0:T(8,128)(2,1)}), bf16[768,4096]{1,0:T(8,128)(2,1)}) %all-gather.5.cloned.1.call-update) | async-done | bytes 6291472 | tf_op jit(solution)/shard_map/all_gather | solution.py:10
  58.5 8.3 %convolution_convert_fusion = bf16[768,512]{1,0:T(8,128)(2,1)} fusion(bf16[768,4096]{1,0:T(8,128)(2,1)} %all-gather.5.cloned.1.call-done, bf16[4096,512]{1,0:T(8,128)(2,1)} %param.10), kind=kOutput, calls=%fused_computation.6 | convolution fusion | flops 3221618688 | bytes 11272192 | tf_op jit(solution)/shard_map/dot_general | solution.py:13
  66.8 0.0 all-gather.7.cloned.1.call-update
  66.9 0.0 all-gather.9.cloned.1.call-start
  66.9 0.7 all-gather.9.cloned.1.call-update
  67.6 46.0 %all-gather.7.cloned.1.call-done = bf16[768,4096]{1,0:T(8,128)(2,1)} async-done(((bf16[768,512]{1,0:T(8,128)(2,1)}), bf16[768,4096]{1,0:T(8,128)(2,1)}) %all-gather.7.cloned.1.call-update) | async-done | bytes 6291472 | tf_op jit(solution)/shard_map/all_gather | solution.py:14
  113.6 6.3 %copy.16 = bf16[96,4,8,1024]{3,2,0,1:T(8,128)(2,1)} copy(bf16[96,4,8,1024]{3,2,1,0:T(8,128)(2,1)} %bitcast.23) | data formatting | bytes 12582912 | tf_op jit(solution)/shard_map/all_to_all | solution.py:16
  119.9 0.0 copy-start.2
  119.9 5.6 %all-to-all-start = ((bf16[768,4,1024]{2,0,1:T(8,128)(2,1)}), bf16[768,4,1024]{2,0,1:T(8,128)(2,1)}, u32[]{:S(2)}, u32[]{:S(2)}) async-start(bf16[768,4,1024]{2,0,1:T(8,128)(2,1)} %bitcast.22), calls=%async_computation | async-start | bytes 12582912 | tf_op jit(solution)/shard_map/all_to_all | solution.py:16
  125.5 0.2 all-gather.11.cloned.1.call-start
  125.8 0.0 copy-done.2
  125.8 0.1 convert_bitcast_fusion
  125.9 0.0 copy-start
  125.9 44.2 %all-gather.9.cloned.1.call-done = bf16[5504,768]{1,0:T(8,128)(2,1)} async-done(((bf16[688,768]{1,0:T(8,128)(2,1)}), bf16[5504,768]{1,0:T(8,128)(2,1)}) %all-gather.9.cloned.1.call-update) | async-done | bytes 8454160 | tf_op jit(solution)/shard_map/all_gather | solution.py:19
  170.1 11.7 %multiply_convert_fusion = bf16[688,768]{1,0:T(8,128)(2,1)} fusion(bf16[688,5504]{1,0:T(8,128)(2,1)} %param.11, bf16[5504,768]{1,0:T(8,128)(2,1)} %all-gather.9.cloned.1.call-done, f32[768]{0:T(1024)S(1)} %convert_bitcast_fusion), kind=kOutput, calls=%fused_computation.4 | convolution fusion | flops 5817507840 | bytes 17087488 | tf_op jit(solution)/shard_map/dot_general | solution.py:17
  181.8 0.0 all-gather.11.cloned.1.call-update
  182.4 0.0 copy-done
  182.4 1.9 broadcast_add_fusion
  184.3 0.0 copy-start.1
  184.3 146.2 %all-gather.11.cloned.1.call-done = bf16[688,3072]{1,0:T(8,128)(2,1)} async-done(((bf16[688,768]{1,0:T(8,128)(2,1)}), bf16[688,3072]{1,0:T(8,128)(2,1)}) %all-gather.11.cloned.1.call-update) | async-done | bytes 4227088 | tf_op jit(solution)/shard_map/all_gather | solution.py:25
  330.6 6.6 %convert_element_type.31 = f32[688,3072]{1,0:T(8,128)} convert(bf16[688,3072]{1,0:T(8,128)(2,1)} %all-gather.11.cloned.1.call-done) | non-fusion elementwise | flops 2113536 | bytes 12681216 | tf_op jit(solution)/shard_map/convert_element_type | solution.py:28
  337.1 0.0 all-to-all-done
  337.1 0.0 copy-done.1
  337.1 22.6 %multiply_reduce_fusion = f32[4,3072]{1,0:T(4,128)S(1)} fusion(f32[688,3072]{1,0:T(8,128)} %convert_element_type.31, bf16[3072,1024,1]{1,0,2:T(8,128)(2,1)} %bitcast.3, bf16[4,688,1024]{2,1,0:T(8,128)(2,1)} %param.12, f32[688,1024]{1,0:T(8,128)S(1)} %copy-done.1), kind=kOutput, calls=%fused_computation | convolution fusion | flops 17339437056 | bytes 23248896 | tf_op jit(solution)/shard_map/td,qjd->qjt/dot_general | solution.py:27
  359.8 0.1 bitcast_reduce_fusion
  359.8 38.4 %psum.7 = f32[24,4]{0,1:T(4,128)S(1)} all-reduce(f32[24,4]{0,1:T(4,128)S(1)} %bitcast.25), channel_id=1, replica_groups=mesh['dp'=4,'tensor'=8] {'dp','tensor'}, use_global_device_ids=true, to_apply=%region_2.3 | all-reduce | flops 96 | bytes 768 | tf_op jit(solution)/shard_map/psum | solution.py:33
  398.2 0.6 dynamic-slice_multiply_fusion
Async XLA Ops:
  6.5 52.0 %all-gather.5.cloned.1.call-start = ((), (), s32[]{:S(2)}) async-start(), calls=%async_computation.1 | async-start | bytes 7077888 | tf_op jit(solution)/shard_map/all_gather | solution.py:10
  7.3 106.3 %all-gather.7.cloned.1.call-start = ((), (), s32[]{:S(2)}) async-start(), calls=%async_computation.2 | async-start | bytes 7077888 | tf_op jit(solution)/shard_map/all_gather | solution.py:14
  66.9 103.2 %all-gather.9.cloned.1.call-start = ((), (), s32[]{:S(2)}) async-start(), calls=%async_computation.3 | async-start | bytes 9510912 | tf_op jit(solution)/shard_map/all_gather | solution.py:19
  119.9 5.9 %copy-start.2 = (s32[6]{0:T(128)S(1)}, s32[6]{0:T(128)}, u32[]{:S(2)}) copy-start(s32[6]{0:T(128)} %param.15) | copy-start | bytes 76
  119.9 217.2 %all-to-all-start = ((bf16[768,4,1024]{2,0,1:T(8,128)(2,1)}), bf16[768,4,1024]{2,0,1:T(8,128)(2,1)}, u32[]{:S(2)}, u32[]{:S(2)}) async-start(bf16[768,4,1024]{2,0,1:T(8,128)(2,1)} %bitcast.22), calls=%async_computation | async-start | bytes 12582912 | tf_op jit(solution)/shard_map/all_to_all | solution.py:16
  125.5 205.0 %all-gather.11.cloned.1.call-start = ((), (), s32[]{:S(2)}) async-start(), calls=%async_computation.4 | async-start | bytes 5283840 | tf_op jit(solution)/shard_map/all_gather | solution.py:25
  125.9 56.6 %copy-start = (f32[688,1024]{1,0:T(8,128)S(1)}, f32[688,1024]{1,0:T(8,128)}, u32[]{:S(2)}) copy-start(f32[688,1024]{1,0:T(8,128)} %param.13) | copy-start | bytes 8454148
  184.3 152.8 %copy-start.1 = (f32[688,1024]{1,0:T(8,128)S(1)}, f32[688,1024]{1,0:T(8,128)}, u32[]{:S(2)}) copy-start(f32[688,1024]{1,0:T(8,128)} %broadcast_add_fusion) | copy-start | bytes 8454148
Sparse Core Ops, SparseCore 0:
  9.2 49.2 all-gather.4
  67.0 46.5 all-gather.6
  115.5 54.5 all-gather.8
  181.9 148.6 all-gather.10
where the time goes:
time: 406 us; the launch traced here: 405 us
  waiting for transfers between devices  289 us (71%)
  matrix products  42.6 us (10%)
  blocking collectives  38.4 us (9%)
  between operations  13.8 us (3%)
  other arithmetic  9.29 us (2%)
  local copies, waits for them, and re-layouts  6.33 us (2%)
  starting transfers between devices  5.92 us (1%)
    all_gather x1, waiting for transfers between devices, local(): grad_proj = lax.all_gather(grad_local, 'dp', axis=1, tiled=True)  146 us
    all_gather x1, waiting for transfers between devices, local(): full_act = lax.all_gather(activations, 'tensor', axis=1, tiled=True)  51.2 us
    all_gather x1, waiting for transfers between devices, local(): act_full = lax.all_gather(act_local, 'tensor', axis=1, tiled=True)  46 us
    all_gather x1, waiting for transfers between devices, local(): lax.all_gather(out_grads_t, 'tensor', axis=0, tiled=True)  44.2 us
    psum x1, blocking collectives, local(): totals = lax.psum(partial_value, ('dp', 'tensor'))  38.4 us
    dot_general x1, matrix products, local(): jnp.einsum('td,qjd->qjt', act_proj, scaled, preferred_element_type=f32)  22.6 us
    dot_general x1, matrix products, local(): jnp.dot(out_basis_t, lax.all_gather(out_grads_t, 'tensor', axis=0, tiled=...  11.7 us
    dot_general x1, matrix products, local(): jnp.dot(full_act, in_basis, preferred_element_type=f32).astype(bf16)  8.3 us
  transfers between devices with their start and end apart: 5, of which 4 were waited for; matrix products, arithmetic and copies ran while one was open for 7% of the time, Pallas kernels for 0%

commit v1 on v0

--- a/solution.py
+++ b/solution.py
@@ -30,7 +30,7 @@
     partial_value = jnp.sum(
         weighted.reshape(query_count, width, tokens // seq_len, seq_len), axis=(1, 3)
     ).T
-    totals = lax.psum(partial_value, ("dp", "tensor"))
+    totals = lax.psum(lax.psum(partial_value, "dp"), "tensor")
     mine = lax.dynamic_slice_in_dim(totals, lax.axis_index("dp") * seq_count, seq_count, 0)
     norm_factor = (features * out_basis_t.shape[1] * seq_len) ** (-0.5)
     return mine * norm_factor

time: 406 us -> 391 us (0.963)
  blocking collectives: 38.4 us -> 23.3 us
    psum x1 -> x2, blocking collectives: 38.4 us -> 23.3 us  [local(): totals = lax.psum(lax.psum(partial_value, 'dp'), 'tensor')]
where the time goes in v1:
time: 391 us; the launch traced here: 390 us
  waiting for transfers between devices  289 us (74%)
  matrix products  42.6 us (11%)
  blocking collectives  23.3 us (6%)
  between operations  13.8 us (4%)
  other arithmetic  9.28 us (2%)
  local copies, waits for them, and re-layouts  6.33 us (2%)
  starting transfers between devices  5.93 us (2%)
    all_gather x1, waiting for transfers between devices, local(): grad_proj = lax.all_gather(grad_local, 'dp', axis=1, tiled=True)  146 us
    all_gather x1, waiting for transfers between devices, local(): full_act = lax.all_gather(activations, 'tensor', axis=1, tiled=True)  51.2 us
    all_gather x1, waiting for transfers between devices, local(): act_full = lax.all_gather(act_local, 'tensor', axis=1, tiled=True)  46 us
    all_gather x1, waiting for transfers between devices, local(): lax.all_gather(out_grads_t, 'tensor', axis=0, tiled=True)  44.2 us
    psum x2, blocking collectives, local(): totals = lax.psum(lax.psum(partial_value, 'dp'), 'tensor')  23.3 us
    dot_general x1, matrix products, local(): jnp.einsum('td,qjd->qjt', act_proj, scaled, preferred_element_type=f32)  22.6 us
    dot_general x1, matrix products, local(): jnp.dot(out_basis_t, lax.all_gather(out_grads_t, 'tensor', axis=0, tiled=...  11.7 us
    dot_general x1, matrix products, local(): jnp.dot(full_act, in_basis, preferred_element_type=f32).astype(bf16)  8.28 us
  transfers between devices with their start and end apart: 5, of which 4 were waited for; matrix products, arithmetic and copies ran while one was open for 7% of the time, Pallas kernels for 0%

profile of v1, /device:TPU:0, one launch (start us, length us, event | category | flops | bytes accessed | tf_op | source)
XLA Modules:
  0.0 390.3 jit_solution(1675297651348862309)
XLA Ops:
  6.5 0.0 all-gather.5.cloned.1.call-start
  6.5 0.7 all-gather.5.cloned.1.call-update
  7.3 0.0 all-gather.7.cloned.1.call-start
  7.3 51.2 %all-gather.5.cloned.1.call-done = bf16[768,4096]{1,0:T(8,128)(2,1)} async-done(((bf16[768,512]{1,0:T(8,128)(2,1)}), bf16[768,4096]{1,0:T(8,128)(2,1)}) %all-gather.5.cloned.1.call-update) | async-done | bytes 6291472 | tf_op jit(solution)/shard_map/all_gather | solution.py:10
  58.5 8.3 %convolution_convert_fusion = bf16[768,512]{1,0:T(8,128)(2,1)} fusion(bf16[768,4096]{1,0:T(8,128)(2,1)} %all-gather.5.cloned.1.call-done, bf16[4096,512]{1,0:T(8,128)(2,1)} %param.10), kind=kOutput, calls=%fused_computation.6 | convolution fusion | flops 3221618688 | bytes 11272192 | tf_op jit(solution)/shard_map/dot_general | solution.py:13
  66.8 0.0 all-gather.7.cloned.1.call-update
  66.8 0.0 all-gather.9.cloned.1.call-start
  66.9 0.7 all-gather.9.cloned.1.call-update
  67.6 46.0 %all-gather.7.cloned.1.call-done = bf16[768,4096]{1,0:T(8,128)(2,1)} async-done(((bf16[768,512]{1,0:T(8,128)(2,1)}), bf16[768,4096]{1,0:T(8,128)(2,1)}) %all-gather.7.cloned.1.call-update) | async-done | bytes 6291472 | tf_op jit(solution)/shard_map/all_gather | solution.py:14
  113.6 6.3 %copy.16 = bf16[96,4,8,1024]{3,2,0,1:T(8,128)(2,1)} copy(bf16[96,4,8,1024]{3,2,1,0:T(8,128)(2,1)} %bitcast.23) | data formatting | bytes 12582912 | tf_op jit(solution)/shard_map/all_to_all | solution.py:16
  119.9 0.0 copy-start.2
  119.9 5.6 %all-to-all-start = ((bf16[768,4,1024]{2,0,1:T(8,128)(2,1)}), bf16[768,4,1024]{2,0,1:T(8,128)(2,1)}, u32[]{:S(2)}, u32[]{:S(2)}) async-start(bf16[768,4,1024]{2,0,1:T(8,128)(2,1)} %bitcast.22), calls=%async_computation | async-start | bytes 12582912 | tf_op jit(solution)/shard_map/all_to_all | solution.py:16
  125.5 0.2 all-gather.11.cloned.1.call-start
  125.8 0.0 copy-done.2
  125.8 0.1 convert_bitcast_fusion
  125.8 0.0 copy-start
  125.8 44.2 %all-gather.9.cloned.1.call-done = bf16[5504,768]{1,0:T(8,128)(2,1)} async-done(((bf16[688,768]{1,0:T(8,128)(2,1)}), bf16[5504,768]{1,0:T(8,128)(2,1)}) %all-gather.9.cloned.1.call-update) | async-done | bytes 8454160 | tf_op jit(solution)/shard_map/all_gather | solution.py:19
  170.0 11.7 %multiply_convert_fusion = bf16[688,768]{1,0:T(8,128)(2,1)} fusion(bf16[688,5504]{1,0:T(8,128)(2,1)} %param.11, bf16[5504,768]{1,0:T(8,128)(2,1)} %all-gather.9.cloned.1.call-done, f32[768]{0:T(1024)S(1)} %convert_bitcast_fusion), kind=kOutput, calls=%fused_computation.4 | convolution fusion | flops 5817507840 | bytes 17087488 | tf_op jit(solution)/shard_map/dot_general | solution.py:17
  181.7 0.0 all-gather.11.cloned.1.call-update
  182.4 0.0 copy-done
  182.4 1.9 broadcast_add_fusion
  184.3 0.0 copy-start.1
  184.3 146.2 %all-gather.11.cloned.1.call-done = bf16[688,3072]{1,0:T(8,128)(2,1)} async-done(((bf16[688,768]{1,0:T(8,128)(2,1)}), bf16[688,3072]{1,0:T(8,128)(2,1)}) %all-gather.11.cloned.1.call-update) | async-done | bytes 4227088 | tf_op jit(solution)/shard_map/all_gather | solution.py:25
  330.5 6.6 %convert_element_type.31 = f32[688,3072]{1,0:T(8,128)} convert(bf16[688,3072]{1,0:T(8,128)(2,1)} %all-gather.11.cloned.1.call-done) | non-fusion elementwise | flops 2113536 | bytes 12681216 | tf_op jit(solution)/shard_map/convert_element_type | solution.py:28
  337.1 0.0 all-to-all-done
  337.1 0.0 copy-done.1
  337.1 22.6 %multiply_reduce_fusion = f32[4,3072]{1,0:T(4,128)S(1)} fusion(f32[688,3072]{1,0:T(8,128)} %convert_element_type.31, bf16[3072,1024,1]{1,0,2:T(8,128)(2,1)} %bitcast.3, bf16[4,688,1024]{2,1,0:T(8,128)(2,1)} %param.12, f32[688,1024]{1,0:T(8,128)S(1)} %copy-done.1), kind=kOutput, calls=%fused_computation | convolution fusion | flops 17339437056 | bytes 23248896 | tf_op jit(solution)/shard_map/td,qjd->qjt/dot_general | solution.py:27
  359.7 0.1 bitcast_reduce_fusion
  359.8 11.5 %psum.14 = f32[24,4]{0,1:T(4,128)S(1)} all-reduce(f32[24,4]{0,1:T(4,128)S(1)} %bitcast.25), channel_id=1, replica_groups=mesh['dp'=4,'tensor'=8] {'dp'}, use_global_device_ids=true, to_apply=%region_2.0 | all-reduce | flops 96 | bytes 768 | tf_op jit(solution)/shard_map/psum | solution.py:33
  371.3 11.8 %psum.15 = f32[24,4]{0,1:T(4,128)S(1)} all-reduce(f32[24,4]{0,1:T(4,128)S(1)} %psum.14), channel_id=1, replica_groups=mesh['dp'=4,'tensor'=8] {'tensor'}, use_global_device_ids=true, to_apply=%region_3.4 | all-reduce | flops 96 | bytes 768 | tf_op jit(solution)/shard_map/psum | solution.py:33
  383.1 0.7 dynamic-slice_multiply_fusion
Async XLA Ops:
  6.5 52.0 %all-gather.5.cloned.1.call-start = ((), (), s32[]{:S(2)}) async-start(), calls=%async_computation.1 | async-start | bytes 7077888 | tf_op jit(solution)/shard_map/all_gather | solution.py:10
  7.3 106.3 %all-gather.7.cloned.1.call-start = ((), (), s32[]{:S(2)}) async-start(), calls=%async_computation.2 | async-start | bytes 7077888 | tf_op jit(solution)/shard_map/all_gather | solution.py:14
  66.8 103.2 %all-gather.9.cloned.1.call-start = ((), (), s32[]{:S(2)}) async-start(), calls=%async_computation.3 | async-start | bytes 9510912 | tf_op jit(solution)/shard_map/all_gather | solution.py:19
  119.9 5.9 %copy-start.2 = (s32[6]{0:T(128)S(1)}, s32[6]{0:T(128)}, u32[]{:S(2)}) copy-start(s32[6]{0:T(128)} %param.15) | copy-start | bytes 76
  119.9 217.2 %all-to-all-start = ((bf16[768,4,1024]{2,0,1:T(8,128)(2,1)}), bf16[768,4,1024]{2,0,1:T(8,128)(2,1)}, u32[]{:S(2)}, u32[]{:S(2)}) async-start(bf16[768,4,1024]{2,0,1:T(8,128)(2,1)} %bitcast.22), calls=%async_computation | async-start | bytes 12582912 | tf_op jit(solution)/shard_map/all_to_all | solution.py:16
  125.5 205.0 %all-gather.11.cloned.1.call-start = ((), (), s32[]{:S(2)}) async-start(), calls=%async_computation.4 | async-start | bytes 5283840 | tf_op jit(solution)/shard_map/all_gather | solution.py:25
  125.8 56.6 %copy-start = (f32[688,1024]{1,0:T(8,128)S(1)}, f32[688,1024]{1,0:T(8,128)}, u32[]{:S(2)}) copy-start(f32[688,1024]{1,0:T(8,128)} %param.13) | copy-start | bytes 8454148
  184.3 152.8 %copy-start.1 = (f32[688,1024]{1,0:T(8,128)S(1)}, f32[688,1024]{1,0:T(8,128)}, u32[]{:S(2)}) copy-start(f32[688,1024]{1,0:T(8,128)} %broadcast_add_fusion) | copy-start | bytes 8454148
Sparse Core Ops, SparseCore 0:
  9.2 49.2 all-gather.4
  67.0 46.5 all-gather.6
  115.5 54.5 all-gather.8
  181.9 148.6 all-gather.10
